TPU v7x, 32 devices: a whole 2x2x4 slice. The times are simulated.
32 devices in a mesh: grp: 8 (over z, y), rep: 2 (over core), tp: 2 (over x).
Axes of the slice: x: 2, y: 2, z: 4, core: 2. Of those that a mesh axis runs over, the one named last changes fastest.
Arguments:
- hidden: bfloat16 [8, 768, 8192], P('grp', 'rep'), may hold values from -6 to 6
- decode_hidden: bfloat16 [8, 2, 2, 32, 8192], P('grp', 'rep'), may hold values from -6 to 6
- norm_gain: bfloat16 [8192], replicated, may hold values from 0.25 to 1.75
- qkv_weight: bfloat16 [8192, 10240], P('grp', 'tp'), may hold values from -0.0625 to 0.0625
- qkv_bias: bfloat16 [10240], P('tp'), may hold values from -32 to 32
- lengths: int32 [8], replicated, may hold values from 12 to 768, as said below
Outputs:
- prefill_out: bfloat16 [8, 768, 8192], P('grp', 'rep', 'tp')
- decode_out: bfloat16 [8, 2, 2, 32, 8192], P('grp', 'rep', None, None, 'tp')
Inputs may be any that keep to these rules, and one draw needn't show every extreme that they name: `lengths`: some prompt is 768 tokens long.
All inputs are finite; a program needn't handle non-finite values.
Results may differ from a plain program's by a relative error of at most 0.012.
The roundings to bfloat16 on the way count: a program that leaves them out, or rounds other values in their place, can miss the bound.
Values may be sent and summed in bfloat16 or wider, within the bound.
A program may use at most 256 MiB of HBM per device.

v0:
```python
import jax
import jax.numpy as jnp
from jax import lax
from jax.sharding import PartitionSpec as P

HD = 128
QPK = 8
STEPS = 4
THETA = 1000000.0
EPSILON = 1e-06
NEGATIVE = -1e30


def shifted(block, axis, distance):
    devices = range(lax.axis_size(axis))
    route = [((i - distance) % len(devices), i) for i in devices]
    return lax.ppermute(block, axis, route)


def normalize(row_block, gain_row):
    widened = row_block.astype(jnp.float32)
    factor = lax.rsqrt(jnp.mean(widened * widened, axis=-1, keepdims=True) + EPSILON)
    return (widened * factor * gain_row.astype(jnp.float32)).astype(jnp.bfloat16)


def rope_tables(positions, head_size):
    half_size = head_size // 2
    frequency = THETA ** (-(jnp.arange(half_size, dtype=jnp.float32) * 2.0 / head_size))
    angle = positions.astype(jnp.float32)[:, None] * frequency[None, :]
    return (jnp.cos(angle), jnp.sin(angle))


def rotate(vector, cosine, sine_part):
    half_size = vector.shape[-1] // 2
    first_half = vector[..., :half_size]
    second = vector[..., half_size:]
    return jnp.concatenate(
        [first_half * cosine - second * sine_part, second * cosine + first_half * sine_part],
        axis=-1,
    )


def masked_max(scores, allowed):
    return jnp.max(jnp.where(allowed, scores, NEGATIVE), axis=-1, keepdims=True)


def combine_values(weight_matrix, value_matrix):
    return jnp.einsum(
        "aprk,kaz->rapz",
        weight_matrix.astype(jnp.bfloat16),
        value_matrix,
        preferred_element_type=jnp.float32,
    )


def pair_scores(query_matrix, key_matrix_rows, score_scale):
    return (
        jnp.einsum(
            "wjro,ujo->jrwu", query_matrix, key_matrix_rows, preferred_element_type=jnp.float32
        )
        * score_scale
    )


def decode_pair(
    query_matrix,
    own_keys,
    own_values,
    prompt_keys,
    prompt_values,
    valid_len,
    local_allowed,
    score_scale,
):
    key_slot_index = jnp.arange(prompt_keys.shape[0], dtype=jnp.int32)
    prompt_allowed = (key_slot_index < valid_len)[None, None, None, :]
    far_scores = pair_scores(query_matrix, prompt_keys, score_scale)
    near_scores = pair_scores(query_matrix, own_keys, score_scale)
    highest = jnp.maximum(
        masked_max(far_scores, prompt_allowed), masked_max(near_scores, local_allowed)
    )
    far_exp = jnp.where(prompt_allowed, jnp.exp(far_scores - highest), 0.0)
    near_exp = jnp.where(local_allowed, jnp.exp(near_scores - highest), 0.0)
    running = jnp.sum(far_exp, axis=-1, keepdims=True) + jnp.sum(near_exp, axis=-1, keepdims=True)
    return combine_values(far_exp / running, prompt_values) + combine_values(
        near_exp / running, own_values
    )


def on_device(hidden, decode_hidden, norm_gain, qkv_weight, qkv_bias, lengths):
    prompt_count = lax.axis_size("grp")
    rep_count = lax.axis_size("rep")
    half_cycle = prompt_count // 2
    grp_here = lax.axis_index("grp")
    rep_here = lax.axis_index("rep")
    span_rows = hidden.shape[1]
    model_width = hidden.shape[2]
    head_block = (QPK + 2) * HD
    heads_here = qkv_bias.shape[0] // head_block
    decode_rows = decode_hidden.shape[3]
    score_scale = HD ** (-0.5)
    prefill_normed = normalize(hidden[0], norm_gain)
    decode_normed = normalize(decode_hidden.reshape(2 * decode_rows, model_width), norm_gain)
    normed = jnp.concatenate([prefill_normed, decode_normed], axis=0)
    share_cols = qkv_weight.shape[1] // rep_count
    own_cols = lax.dynamic_slice_in_dim(qkv_weight, rep_here * share_cols, share_cols, 1)
    columns = lax.all_gather(own_cols, "grp", axis=0, tiled=True)
    complete = lax.all_gather(columns, "rep", axis=1, tiled=True)
    projected = jnp.dot(normed, complete, preferred_element_type=jnp.float32)
    projected = (projected + qkv_bias.astype(jnp.float32)).reshape(
        normed.shape[0], heads_here, QPK + 2, HD
    )
    index_table = jnp.arange(prompt_count, dtype=jnp.int32)

    def length_of(prompt):
        return jnp.sum(jnp.where(index_table == prompt, lengths, 0))

    own_len = length_of(grp_here)
    far_len = length_of((grp_here + half_cycle) % prompt_count)
    row_position = rep_here * span_rows + jnp.arange(span_rows, dtype=jnp.int32)
    local_ids = jnp.arange(decode_rows, dtype=jnp.int32)
    step_ids = local_ids % STEPS
    sample_ids = local_ids // STEPS
    positions = jnp.concatenate([row_position, own_len + step_ids, far_len + step_ids])
    cosine, sine_part = rope_tables(positions, HD)
    query_matrix = rotate(
        projected[:, :, :QPK], cosine[:, None, None, :], sine_part[:, None, None, :]
    ).astype(jnp.bfloat16)
    key_matrix_rows = rotate(
        projected[:, :, QPK], cosine[:, None, :], sine_part[:, None, :]
    ).astype(jnp.bfloat16)
    value_matrix = projected[:, :, QPK + 1].astype(jnp.bfloat16)
    cache_keys, cache_values = (
        lax.all_gather(key_matrix_rows[:span_rows], "rep", axis=0, tiled=True),
        lax.all_gather(value_matrix[:span_rows], "rep", axis=0, tiled=True),
    )
    key_pos = jnp.arange(cache_keys.shape[0], dtype=jnp.int32)
    allowed = ((key_pos[None, :] <= row_position[:, None]) & (key_pos[None, :] < own_len))[
        None, None
    ]
    scores = pair_scores(query_matrix[:span_rows], cache_keys, score_scale)
    highest = masked_max(scores, allowed)
    exponent = jnp.where(allowed, jnp.exp(scores - highest), 0.0)
    weight_matrix = exponent / jnp.sum(exponent, axis=-1, keepdims=True)
    attended = combine_values(weight_matrix, cache_values)
    prefill_out = attended.astype(jnp.bfloat16).reshape(1, span_rows, heads_here * QPK * HD)
    decode_queries = query_matrix[span_rows:].reshape(2, decode_rows, heads_here, QPK, HD)
    decode_keys = key_matrix_rows[span_rows:].reshape(2, decode_rows, heads_here, HD)
    decode_values = value_matrix[span_rows:].reshape(2, decode_rows, heads_here, HD)
    local_allowed = (
        (sample_ids[None, :] == sample_ids[:, None]) & (step_ids[None, :] <= step_ids[:, None])
    )[None, None]
    near_out = decode_pair(
        decode_queries[0],
        decode_keys[0],
        decode_values[0],
        cache_keys,
        cache_values,
        own_len,
        local_allowed,
        score_scale,
    )
    far_keys, far_values = shifted((cache_keys, cache_values), "grp", half_cycle)
    far_out = decode_pair(
        decode_queries[1],
        decode_keys[1],
        decode_values[1],
        far_keys,
        far_values,
        far_len,
        local_allowed,
        score_scale,
    )
    decode_out = (
        jnp.stack([near_out, far_out])
        .astype(jnp.bfloat16)
        .reshape(1, 1, 2, decode_rows, heads_here * QPK * HD)
    )
    return (prefill_out, decode_out)


def solution(mesh):
    return jax.shard_map(
        on_device,
        mesh=mesh,
        in_specs=(
            P("grp", "rep", None),
            P("grp", "rep", None, None, None),
            P(),
            P("grp", "tp"),
            P("tp"),
            P(),
        ),
        out_specs=(P("grp", "rep", "tp"), P("grp", "rep", None, None, "tp")),
        check_vma=False,
    )
```

profile of v0, /device:TPU:0, one launch (start us, length us, event | category | flops | bytes accessed | tf_op | source)
XLA Modules:
  0.0 1132.9 jit_solution(10912499802913706107)
XLA Ops:
  7.2 0.0 all-gather.4.cloned.1.call-start
  7.2 5.1 constant_dynamic-slice_fusion
  12.4 0.0 all-gather.4.cloned.1.call-update
  12.4 0.0 all-gather.6.cloned.1.call-start
  12.4 797.8 %all-gather.4.cloned.1.call-done = bf16[8192,2560]{1,0:T(8,128)(2,1)} async-done(((bf16[1024,2560]{1,0:T(8,128)(2,1)}), bf16[8192,2560]{1,0:T(8,128)(2,1)}) %all-gather.4.cloned.1.call-update) | async-done | bytes 41943056 | tf_op jit(solution)/shard_map/all_gather | solution.py:107
  810.2 0.0 all-gather.6.cloned.1.call-update
  810.3 0.7 copy-done.10
  810.9 0.5 copy-done.7
  811.5 0.3 multiply_reduce_fusion
  811.8 0.1 rsqrt.21
  811.9 0.6 fusion.74
  812.6 0.6 iota_compare_fusion.2
  813.2 1.3 broadcast_add_fusion
  814.5 1.2 iota_compare_fusion.1
  815.7 0.1 add_convert_fusion.2
  815.8 4.9 fusion.9
  820.8 0.7 compare_and_fusion
  821.4 0.9 fusion.40
  822.4 0.9 multiply_cosine_fusion
  823.3 0.3 fusion.32
  823.6 12.1 %fusion.11 = bf16[384,8192]{1,0:T(8,128)(2,1)} fusion(bf16[1,384,8192]{2,1,0:T(8,128)(2,1)} %param.6, f32[8192]{0:T(1024)S(1)} %convert_element_type.70, f32[384]{0:T(512)S(1)} %add_rsqrt_fusion), kind=kLoop, calls=%fused_computation.16 | loop fusion | flops 12582912 | bytes 12617216 | tf_op jit(solution)/shard_map/convert_element_type | solution.py:23
  835.6 95.3 %all-gather.6.cloned.1.call-done = bf16[8192,5120]{1,0:T(8,128)(2,1)} async-done(((bf16[8192,2560]{1,0:T(8,128)(2,1)}), bf16[8192,5120]{1,0:T(8,128)(2,1)}) %all-gather.6.cloned.1.call-update) | async-done | bytes 83886096 | tf_op jit(solution)/shard_map/all_gather | solution.py:108
  931.0 47.5 %fusion.16 = f32[448,5120]{1,0:T(8,128)} fusion(bf16[8192,5120]{1,0:T(8,128)(2,1)} %all-gather.6.cloned.1.call-done, bf16[64,8192]{1,0:T(8,128)(2,1)S(1)} %fusion.32, bf16[384,8192]{1,0:T(8,128)(2,1)} %fusion.11, f32[5120]{0:T(1024)S(1)} %convert_element_type.76), kind=kOutput, calls=%fused_computation.24 | convolution fusion | flops 37597937664 | bytes 100421632 | tf_op jit(solution)/shard_map/dot_general | solution.py:109
  978.5 10.8 copy.20
  989.3 1.3 slice.92
  990.6 8.8 fusion.92
  999.4 3.1 copy.59
  1002.5 0.3 copy.55
  1002.8 0.4 add_convert_fusion.1
  1003.2 0.0 copy-start.3
  1003.2 0.7 copy-done.3
  1004.0 0.2 fusion.59
  1004.2 2.5 all_gather.15
  1006.7 6.5 copy.56
  1013.2 6.5 copy.57
  1019.7 6.3 add_convert_fusion
  1026.1 0.1 pad_maximum_fusion.1
  1026.3 1.6 copy-done.1
  1027.9 1.1 copy-done.2
  1029.0 1.9 fusion.25
  1030.9 2.7 collective-permute-start.1
  1033.6 26.4 %fusion.93 = (f32[4,8,384]{2,1,0:T(8,128)S(1)}, f32[4,8,384,768]{2,3,1,0:T(8,128)}) fusion(pred[384,768]{0,1:T(8,128)(4,1)} %fusion.40, bf16[768,4,128]{2,0,1:T(8,128)(2,1)} %all_gather.15, bf16[448,4,8,64]{3,0,2,1:T(8,128)(2,1)} %copy-done.2, bf16[448,4,8,64]{3,0,2,1:T(8,128)(2,1)} %copy-done.1), kind=kOutput, calls=%fused_computation.139 | convolution fusion | flops 4901044736 | bytes 54640640 | tf_op jit(solution)/shard_map/sub | solution.py:143
  1060.0 1.0 slice.91
  1061.1 2.5 all-gather
  1063.6 15.2 %fusion.30 = bf16[4,128,8,384]{3,1,2,0:T(8,128)(2,1)} fusion(f32[4,8,384,768]{2,3,1,0:T(8,128)} %get-tuple-element.19, f32[4,8,384]{2,1,0:T(8,128)S(1)} %get-tuple-element.18, bf16[768,4,1,128]{0,3,1,2:T(8,128)(2,1)} %all-gather), kind=kOutput, calls=%fused_computation.45 | convolution fusion | flops 2436366336 | bytes 41730048 | tf_op jit(solution)/shard_map/aprk,kaz->rapz/dot_general | solution.py:48
  1078.8 4.6 copy.34
  1083.5 1.8 select_reduce_fusion.1
  1085.2 0.3 collective-permute-start
  1085.6 0.8 fusion.28
  1086.4 1.4 fusion.57
  1087.8 2.1 fusion.33
  1089.9 0.0 copy-start.8
  1089.9 1.3 fusion.41
  1091.2 0.1 copy.29
  1091.3 0.1 stack.9
  1091.4 1.8 fusion.22
  1093.2 0.1 fusion.58
  1093.4 0.8 fusion.29
  1094.2 1.3 fusion.64
  1095.5 27.3 %collective-permute-done = bf16[768,4,128]{0,2,1:T(8,128)(2,1)} collective-permute-done((bf16[768,4,128]{0,2,1:T(8,128)(2,1)}, bf16[768,4,128]{0,2,1:T(8,128)(2,1)}, u32[]{:S(2)}, u32[]{:S(2)}) %collective-permute-start) | collective-permute-done | bytes 786464 | tf_op jit(solution)/shard_map/ppermute | solution.py:17
  1122.9 2.2 fusion.42
  1125.0 0.1 copy.33
  1125.1 0.1 stack.10
  1125.3 0.8 pad_maximum_fusion
  (33 shorter events, 0.1 us)
Async XLA Ops:
  7.2 803.1 %all-gather.4.cloned.1.call-start = ((), (), s32[]{:S(2)}) async-start(), calls=%async_computation | async-start | bytes 47185920 | tf_op jit(solution)/shard_map/all_gather | solution.py:107
  12.4 918.6 %all-gather.6.cloned.1.call-start = ((), (), s32[]{:S(2)}) async-start(), calls=%async_computation.1 | async-start | bytes 125829120 | tf_op jit(solution)/shard_map/all_gather | solution.py:108
  810.2 0.7 copy-start.10
  810.2 1.2 copy-start.7
  810.2 1.6 copy-start.11
  810.2 1.7 copy-start.13
  990.6 8.8 copy-start
  1003.2 0.8 copy-start.3
  1003.2 1.0 copy-start.5
  1026.1 1.8 copy-start.1
  1026.1 2.9 copy-start.2
  1030.9 60.5 %collective-permute-start.1 = (bf16[768,4,128]{2,0,1:T(8,128)(2,1)}, bf16[768,4,128]{2,0,1:T(8,128)(2,1)}, u32[]{:S(2)}, u32[]{:S(2)}) collective-permute-start(bf16[768,4,128]{2,0,1:T(8,128)(2,1)} %all_gather.15), channel_id=1, source_target_pairs={{16,0},{20,4},{24,8},{28,12},{0,16},{4,20},{8,24},{12,28},{17,1},{... | collective-permute-start | bytes 2359304 | tf_op jit(solution)/shard_map/ppermute | solution.py:17
  1078.8 4.6 copy-start.9
  1083.5 2.9 copy-start.4
  1083.5 2.9 copy-start.6
  1085.2 37.6 %collective-permute-start = (bf16[768,4,128]{0,2,1:T(8,128)(2,1)}, bf16[768,4,128]{0,2,1:T(8,128)(2,1)}, u32[]{:S(2)}, u32[]{:S(2)}) collective-permute-start(bf16[768,4,128]{0,2,1:T(8,128)(2,1)} %bitcast.4), channel_id=1, source_target_pairs={{16,0},{20,4},{24,8},{28,12},{0,16},{4,20},{8,24},{12,28},{17,1},{... | collective-permute-start | bytes 2359304 | tf_op jit(solution)/shard_map/ppermute | solution.py:17
  1087.8 3.6 copy-start.12
  1089.9 3.4 copy-start.8
Sparse Core Ops, SparseCore 0:
  12.5 797.6 all-gather.3
  811.8 119.1 all-gather.5
where the time goes:
time: 1130 us
  waiting for transfers between devices  921 us (82%)
  matrix products  103 us (9%)
  local copies, waits for them, and re-layouts  53.4 us (5%)
  other arithmetic  33.8 us (3%)
  between operations  14.4 us (1%)
    all_gather x1, waiting for transfers between devices, on_device(): columns = lax.all_gather(own_cols, 'grp', axis=0, tiled=True)  798 us
    all_gather x1, waiting for transfers between devices, on_device(): complete = lax.all_gather(columns, 'rep', axis=1, tiled=True)  95.3 us
    dot_general x1, matrix products, on_device(): projected = jnp.dot(normed, complete, preferred_element_type=jnp.float32)  47.5 us
    ppermute x2, waiting for transfers between devices, shifted(): return lax.ppermute(block, axis, route)  27.4 us
    sub x1, matrix products, on_device(): exponent = jnp.where(allowed, jnp.exp(scores - highest), 0.0)  26.4 us
    unnamed x32, local copies, waits for them, and re-layouts  22.7 us
  transfers between devices with their start and end apart: 4, of which 3 were waited for; matrix products, arithmetic and copies ran while one was open for 7% of the time, Pallas kernels for 0%

commit v1 on v0

--- a/solution.py
+++ b/solution.py
@@ -9,6 +9,19 @@
 THETA = 1000000.0
 EPSILON = 1e-06
 NEGATIVE = -1e30
+
+
+def gather_around(shard, axis, dim):
+    ways = lax.axis_size(axis)
+    up = [(d, (d + 1) % ways) for d in range(ways)]
+    down = [(d, (d - 1) % ways) for d in range(ways)]
+    earlier, later = ([shard], [shard])
+    for _ in range(ways // 2):
+        earlier.append(lax.ppermute(earlier[-1], axis, up))
+    for _ in range((ways - 1) // 2):
+        later.append(lax.ppermute(later[-1], axis, down))
+    line = jnp.concatenate([*earlier[::-1], *later[1:]], axis=dim)
+    return jnp.roll(line, (lax.axis_index(axis) - ways // 2) * shard.shape[dim], axis=dim)
 
 
 def shifted(block, axis, distance):
@@ -104,7 +117,7 @@
     normed = jnp.concatenate([prefill_normed, decode_normed], axis=0)
     share_cols = qkv_weight.shape[1] // rep_count
     own_cols = lax.dynamic_slice_in_dim(qkv_weight, rep_here * share_cols, share_cols, 1)
-    columns = lax.all_gather(own_cols, "grp", axis=0, tiled=True)
+    columns = gather_around(own_cols, "grp", 0)
     complete = lax.all_gather(columns, "rep", axis=1, tiled=True)
     projected = jnp.dot(normed, complete, preferred_element_type=jnp.float32)
     projected = (projected + qkv_bias.astype(jnp.float32)).reshape(

time: 1130 us -> 1210 us (1.071); the launches traced: 1130 us -> 1200 us
  waiting for transfers between devices: 921 us -> 656 us
  starting transfers between devices: 3.13 us -> 246 us
  local copies, waits for them, and re-layouts: 53.4 us -> 148 us
    all_gather x1 -> x0, waiting for transfers between devices: 798 us -> none  [on_device(): columns = lax.all_gather(own_cols, 'grp', axis=0, tiled=True)]
    ppermute x0 -> x7, waiting for transfers between devices: none -> 552 us  [the longest x4 550 us: gather_around(): earlier.append(lax.ppermute(earlier[-1], axis, up))]
    ppermute x0 -> x7, starting transfers between devices: none -> 241 us  [the longest x3 233 us: gather_around(): later.append(lax.ppermute(later[-1], axis, down))]
    unnamed x32 -> x63, local copies, waits for them, and re-layouts: 22.7 us -> 87 us
    dynamic_slice x0 -> x1, local copies, waits for them, and re-layouts: none -> 29 us  [gather_around(): jnp.roll(line, (lax.axis_index(axis) - ways // 2) * shard.shape[dim], axi...]
    ppermute x2, waiting for transfers between devices: 27.4 us -> 11.7 us  [shifted(): return lax.ppermute(block, axis, route)]
  transfers between devices with their start and end apart: 4 -> 10, of which waited for: 3 -> 7; matrix products, arithmetic and copies ran while one was open for 7% -> 9% of each run, Pallas kernels for 0% -> 0%
where the time goes in v1:
time: 1210 us; the launch traced here: 1200 us
  waiting for transfers between devices  656 us (54%)
  starting transfers between devices  246 us (20%)
  local copies, waits for them, and re-layouts  148 us (12%)
  matrix products  95.3 us (8%)
  other arithmetic  34.4 us (3%)
  between operations  14.6 us (1%)
    ppermute x4, waiting for transfers between devices, gather_around(): earlier.append(lax.ppermute(earlier[-1], axis, up))  550 us
    ppermute x3, starting transfers between devices, gather_around(): later.append(lax.ppermute(later[-1], axis, down))  233 us
    all_gather x1, waiting for transfers between devices, on_device(): complete = lax.all_gather(columns, 'rep', axis=1, tiled=True)  92 us
    unnamed x63, local copies, waits for them, and re-layouts  87 us
    dot_general x1, matrix products, on_device(): projected = jnp.dot(normed, complete, preferred_element_type=jnp.float32)  47.7 us
    dynamic_slice x1, local copies, waits for them, and re-layouts, gather_around(): jnp.roll(line, (lax.axis_index(axis) - ways // 2) * shard.shape[dim], axi...  29 us
    sub x1, matrix products, on_device(): exponent = jnp.where(allowed, jnp.exp(scores - highest), 0.0)  24.2 us
  transfers between devices with their start and end apart: 10, of which 7 were waited for; matrix products, arithmetic and copies ran while one was open for 9% of the time, Pallas kernels for 0%

profile of v1, /device:TPU:0, one launch (start us, length us, event | category | flops | bytes accessed | tf_op | source)
XLA Modules:
  0.0 1199.0 jit_solution(7161930958652726977)
XLA Ops:
  7.2 2.8 constant_dynamic-slice_fusion.1
  10.0 3.0 collective-permute-start
  13.1 116.1 %collective-permute-done = bf16[1024,2560]{1,0:T(8,128)(2,1)S(1)} collective-permute-done((bf16[1024,2560]{1,0:T(8,128)(2,1)S(1)}, bf16[1024,2560]{1,0:T(8,128)(2,1)S(1)}, u32[]{:S(2)}, u32[]{:S(2)}) %collective-permute-start) | collective-permute-done | bytes 5242912 | tf_op jit(solution)/shard_map/ppermute | solution.py:20
  129.2 2.3 copy-done.3
  131.4 4.7 collective-permute-start.4
  136.2 219.6 %collective-permute-done.1 = bf16[1024,2560]{1,0:T(8,128)(2,1)S(1)} collective-permute-done((bf16[1024,2560]{1,0:T(8,128)(2,1)S(1)}, bf16[1024,2560]{1,0:T(8,128)(2,1)S(1)}, u32[]{:S(2)}, u32[]{:S(2)}) %collective-permute-start.1) | collective-permute-done | bytes 5242912 | tf_op jit(solution)/shard_map/ppermute | solution.py:20
  355.8 2.5 collective-permute-start.2
  358.3 2.4 copy-done.4
  360.7 113.3 %collective-permute-start.5 = (bf16[1024,2560]{1,0:T(8,128)(2,1)S(1)}, bf16[1024,2560]{1,0:T(8,128)(2,1)}, u32[]{:S(2)}, u32[]{:S(2)}) collective-permute-start(bf16[1024,2560]{1,0:T(8,128)(2,1)S(1)} %collective-permute-done.4), channel_id=1, source_target_pairs={{0,28},{4,0},{8,4},{12,8},{16,12},{20,16},{24,20},{28,24},{1,29},{... | collective-permute-start | bytes 15728648 | tf_op jit(solution)/shard_map/ppermute | solution.py:22
  474.0 107.9 %collective-permute-done.2 = bf16[1024,2560]{1,0:T(8,128)(2,1)} collective-permute-done((bf16[1024,2560]{1,0:T(8,128)(2,1)S(1)}, bf16[1024,2560]{1,0:T(8,128)(2,1)}, u32[]{:S(2)}, u32[]{:S(2)}) %collective-permute-start.2) | collective-permute-done | bytes 5242912 | tf_op jit(solution)/shard_map/ppermute | solution.py:20
  582.0 2.6 collective-permute-start.3
  584.5 2.0 collective-permute-done.5
  586.5 114.8 %collective-permute-start.6 = (bf16[1024,2560]{1,0:T(8,128)(2,1)}, bf16[1024,2560]{1,0:T(8,128)(2,1)}, u32[]{:S(2)}, u32[]{:S(2)}) collective-permute-start(bf16[1024,2560]{1,0:T(8,128)(2,1)} %collective-permute-done.5), channel_id=1, source_target_pairs={{0,28},{4,0},{8,4},{12,8},{16,12},{20,16},{24,20},{28,24},{1,29},{... | collective-permute-start | bytes 15728648 | tf_op jit(solution)/shard_map/ppermute | solution.py:22
  701.4 106.3 %collective-permute-done.3 = bf16[1024,2560]{1,0:T(8,128)(2,1)} collective-permute-done((bf16[1024,2560]{1,0:T(8,128)(2,1)}, bf16[1024,2560]{1,0:T(8,128)(2,1)}, u32[]{:S(2)}, u32[]{:S(2)}) %collective-permute-start.3) | collective-permute-done | bytes 5242912 | tf_op jit(solution)/shard_map/ppermute | solution.py:20
  807.7 5.6 constant_dynamic-update-slice_fusion.15
  813.3 5.4 constant_dynamic-update-slice_fusion.14
  818.7 3.0 constant_dynamic-update-slice_fusion.13
  821.8 3.0 constant_dynamic-update-slice_fusion.12
  824.8 1.2 slice-done.1
  826.0 0.8 slice-done.2
  826.8 2.7 constant_dynamic-update-slice_fusion.11
  829.5 2.7 constant_dynamic-update-slice_fusion.10
  832.2 5.1 constant_dynamic-update-slice_fusion.9
  837.4 5.1 constant_dynamic-update-slice_fusion.8
  842.5 5.2 constant_dynamic-update-slice_fusion.7
  847.6 5.1 constant_dynamic-update-slice_fusion.6
  852.7 5.1 constant_dynamic-update-slice_fusion.5
  857.8 2.6 constant_dynamic-update-slice_fusion.4
  860.4 2.7 constant_dynamic-update-slice_fusion.3
  863.1 2.7 constant_dynamic-update-slice_fusion.2
  865.8 5.1 constant_dynamic-update-slice_fusion.1
  870.9 5.2 constant_dynamic-update-slice_fusion
  876.1 29.0 %constant_dynamic-slice_fusion = bf16[8192,2560]{1,0:T(8,128)(2,1)} fusion(bf16[16384,2560]{1,0:T(8,128)(2,1)} %constant_dynamic-update-slice_fusion, s32[]{:T(128)S(6)} %select_n.111), kind=kLoop, calls=%fused_computation.140 | loop fusion | bytes 83886080 | tf_op jit(solution)/shard_map/jit(_roll_dynamic)/dynamic_slice | solution.py:24
  908.1 1.3 broadcast_add_fusion
  909.4 1.3 iota_compare_fusion.1
  910.7 6.1 fusion.9
  916.9 1.0 fusion.40
  917.8 0.9 multiply_cosine_fusion
  919.0 12.1 %fusion.11 = bf16[384,8192]{1,0:T(8,128)(2,1)} fusion(bf16[1,384,8192]{2,1,0:T(8,128)(2,1)} %param.6, f32[8192]{0:T(1024)S(1)} %convert_element_type.70, f32[384]{0:T(512)S(1)} %add_rsqrt_fusion), kind=kLoop, calls=%fused_computation.16 | loop fusion | flops 12582912 | bytes 12617216 | tf_op jit(solution)/shard_map/convert_element_type | solution.py:36
  931.1 92.0 %all-gather.3.cloned.1.call-done = bf16[8192,5120]{1,0:T(8,128)(2,1)} async-done(((bf16[8192,2560]{1,0:T(8,128)(2,1)}), bf16[8192,5120]{1,0:T(8,128)(2,1)}) %all-gather.3.cloned.1.call-update) | async-done | bytes 83886096 | tf_op jit(solution)/shard_map/all_gather | solution.py:121
  1023.2 47.7 %fusion.16 = f32[448,5120]{1,0:T(8,128)} fusion(bf16[8192,5120]{1,0:T(8,128)(2,1)} %all-gather.3.cloned.1.call-done, bf16[64,8192]{1,0:T(8,128)(2,1)S(1)} %fusion.32, bf16[384,8192]{1,0:T(8,128)(2,1)} %fusion.11, f32[5120]{0:T(1024)S(1)} %convert_element_type.76), kind=kOutput, calls=%fused_computation.24 | convolution fusion | flops 37597937664 | bytes 100421632 | tf_op jit(solution)/shard_map/dot_general | solution.py:122
  1070.8 11.0 copy.20
  1081.8 8.7 fusion.92
  1090.6 3.1 copy.59
  1093.7 6.5 copy.56
  1100.2 6.5 copy.57
  1107.6 2.4 all_gather.11
  1110.0 6.3 add_convert_fusion
  1116.5 0.8 fusion.25
  1117.2 2.7 collective-permute-start.8
  1120.6 1.0 slice.91
  1121.7 2.4 all-gather
  1124.0 0.8 fusion.28
  1125.5 1.0 fusion.33
  1126.5 1.2 fusion.41
  1128.0 2.0 collective-permute-start.7
  1129.9 24.2 %fusion.93 = (f32[4,8,384]{2,1,0:T(8,128)S(1)}, f32[4,8,384,768]{2,3,1,0:T(8,128)}) fusion(pred[384,768]{0,1:T(8,128)(4,1)S(1)} %copy-done.8, bf16[768,4,128]{2,0,1:T(8,128)(2,1)S(1)} %all_gather.11, bf16[448,4,8,64]{3,0,2,1:T(8,128)(2,1)} %copy-done.2, bf16[448,4,8,64]{3,0,2,1:T(8,128)(2,1)} %copy-done.1), kind=kOutput, calls=%fused_computation.156 | convolution fusion | flops 4901044736 | bytes 54640640 | tf_op jit(solution)/shard_map/sub | solution.py:156
  1154.2 15.2 %fusion.30 = bf16[4,128,8,384]{3,1,2,0:T(8,128)(2,1)} fusion(f32[4,8,384,768]{2,3,1,0:T(8,128)} %get-tuple-element.19, f32[4,8,384]{2,1,0:T(8,128)S(1)} %get-tuple-element.18, bf16[768,4,1,128]{0,3,1,2:T(8,128)(2,1)} %copy-done.7), kind=kOutput, calls=%fused_computation.45 | convolution fusion | flops 2436366336 | bytes 41730048 | tf_op jit(solution)/shard_map/aprk,kaz->rapz/dot_general | solution.py:61
  1169.4 4.6 copy.34
  1174.8 0.8 fusion.29
  1175.7 1.3 fusion.64
  1176.9 11.7 collective-permute-done.7
  1188.7 2.2 fusion.42
  1191.1 0.8 pad_maximum_fusion
  (81 shorter events, 7.1 us)
Async XLA Ops:
  7.2 1016.0 %all-gather.3.cloned.1.call-start = ((), (), s32[]{:S(2)}) async-start(), calls=%async_computation | async-start | bytes 125829120 | tf_op jit(solution)/shard_map/all_gather | solution.py:121
  10.0 119.1 %collective-permute-start = (bf16[1024,2560]{1,0:T(8,128)(2,1)S(1)}, bf16[1024,2560]{1,0:T(8,128)(2,1)S(1)}, u32[]{:S(2)}, u32[]{:S(2)}) collective-permute-start(bf16[1024,2560]{1,0:T(8,128)(2,1)S(1)} %constant_dynamic-slice_fusion.1), channel_id=1, source_target_pairs={{0,4},{4,8},{8,12},{12,16},{16,20},{20,24},{24,28},{28,0},{1,5},{5... | collective-permute-start | bytes 15728648 | tf_op jit(solution)/shard_map/ppermute | solution.py:20
  129.2 2.3 copy-start.3
  131.4 224.4 %collective-permute-start.1 = (bf16[1024,2560]{1,0:T(8,128)(2,1)S(1)}, bf16[1024,2560]{1,0:T(8,128)(2,1)S(1)}, u32[]{:S(2)}, u32[]{:S(2)}) collective-permute-start(bf16[1024,2560]{1,0:T(8,128)(2,1)S(1)} %collective-permute-done), channel_id=1, source_target_pairs={{0,4},{4,8},{8,12},{12,16},{16,20},{20,24},{24,28},{28,0},{1,5},{5... | collective-permute-start | bytes 15728648 | tf_op jit(solution)/shard_map/ppermute | solution.py:20
  131.4 226.8 %collective-permute-start.4 = (bf16[1024,2560]{1,0:T(8,128)(2,1)S(1)}, bf16[1024,2560]{1,0:T(8,128)(2,1)S(1)}, u32[]{:S(2)}, u32[]{:S(2)}) collective-permute-start(bf16[1024,2560]{1,0:T(8,128)(2,1)S(1)} %constant_dynamic-slice_fusion.1), channel_id=1, source_target_pairs={{0,28},{4,0},{8,4},{12,8},{16,12},{20,16},{24,20},{28,24},{1,29},{... | collective-permute-start | bytes 15728648 | tf_op jit(solution)/shard_map/ppermute | solution.py:22
  355.8 230.7 %copy-start.5 = (bf16[1024,2560]{1,0:T(8,128)(2,1)}, bf16[1024,2560]{1,0:T(8,128)(2,1)S(1)}, u32[]{:S(2)}) copy-start(bf16[1024,2560]{1,0:T(8,128)(2,1)S(1)} %collective-permute-done.1) | copy-start | bytes 15728644
  355.8 226.1 %collective-permute-start.2 = (bf16[1024,2560]{1,0:T(8,128)(2,1)S(1)}, bf16[1024,2560]{1,0:T(8,128)(2,1)}, u32[]{:S(2)}, u32[]{:S(2)}) collective-permute-start(bf16[1024,2560]{1,0:T(8,128)(2,1)S(1)} %collective-permute-done.1), channel_id=1, source_target_pairs={{0,4},{4,8},{8,12},{12,16},{16,20},{20,24},{24,28},{28,0},{1,5},{5... | collective-permute-start | bytes 15728648 | tf_op jit(solution)/shard_map/ppermute | solution.py:20
  358.3 2.4 copy-start.4
  360.7 225.8 %collective-permute-start.5 = (bf16[1024,2560]{1,0:T(8,128)(2,1)S(1)}, bf16[1024,2560]{1,0:T(8,128)(2,1)}, u32[]{:S(2)}, u32[]{:S(2)}) collective-permute-start(bf16[1024,2560]{1,0:T(8,128)(2,1)S(1)} %collective-permute-done.4), channel_id=1, source_target_pairs={{0,28},{4,0},{8,4},{12,8},{16,12},{20,16},{24,20},{28,24},{1,29},{... | collective-permute-start | bytes 15728648 | tf_op jit(solution)/shard_map/ppermute | solution.py:22
  582.0 225.7 %collective-permute-start.3 = (bf16[1024,2560]{1,0:T(8,128)(2,1)}, bf16[1024,2560]{1,0:T(8,128)(2,1)}, u32[]{:S(2)}, u32[]{:S(2)}) collective-permute-start(bf16[1024,2560]{1,0:T(8,128)(2,1)} %collective-permute-done.2), channel_id=1, source_target_pairs={{0,4},{4,8},{8,12},{12,16},{16,20},{20,24},{24,28},{28,0},{1,5},{5... | collective-permute-start | bytes 15728648 | tf_op jit(solution)/shard_map/ppermute | solution.py:20
  586.5 250.8 %collective-permute-start.6 = (bf16[1024,2560]{1,0:T(8,128)(2,1)}, bf16[1024,2560]{1,0:T(8,128)(2,1)}, u32[]{:S(2)}, u32[]{:S(2)}) collective-permute-start(bf16[1024,2560]{1,0:T(8,128)(2,1)} %collective-permute-done.5), channel_id=1, source_target_pairs={{0,28},{4,0},{8,4},{12,8},{16,12},{20,16},{24,20},{28,24},{1,29},{... | collective-permute-start | bytes 15728648 | tf_op jit(solution)/shard_map/ppermute | solution.py:22
  807.7 11.1 slice-start.7
  807.7 14.1 %slice-start.3 = ((s8[5242880]{0:T(1024)(128)(4,1)}), s8[4194304]{0:T(1024)(128)(4,1)S(1)}, s32[]{:S(2)}) async-start(s8[5242880]{0:T(1024)(128)(4,1)} %bitcast.154), calls=%async_computation.4 | async-start | bytes 8388608
  813.3 5.4 slice-start.8
  813.3 8.5 slice-start.4
  818.7 6.0 slice-start
  818.7 7.2 slice-start.1
  821.8 5.1 slice-start.2
  821.8 7.8 slice-start.5
  826.8 2.7 slice-start.6
  905.1 0.7 copy-start.9
  905.1 1.2 copy-start.6
  905.1 1.6 copy-start.10
  905.1 1.7 copy-start.12
  1081.8 8.7 copy-start
  1116.3 3.7 copy-start.1
  1116.3 3.7 copy-start.2
  1117.2 56.7 %collective-permute-start.8 = (bf16[768,4,128]{2,0,1:T(8,128)(2,1)S(1)}, bf16[768,4,128]{2,0,1:T(8,128)(2,1)S(1)}, u32[]{:S(2)}, u32[]{:S(2)}) collective-permute-start(bf16[768,4,128]{2,0,1:T(8,128)(2,1)S(1)} %all_gather.11), channel_id=1, source_target_pairs={{16,0},{20,4},{24,8},{28,12},{0,16},{4,20},{8,24},{12,28},{17,1},{... | collective-permute-start | bytes 2359304 | tf_op jit(solution)/shard_map/ppermute | solution.py:30
  1124.0 2.5 copy-start.7
  1125.5 4.5 copy-start.8
  1128.0 60.7 %collective-permute-start.7 = (bf16[768,4,128]{0,2,1:T(8,128)(2,1)}, bf16[768,4,128]{0,2,1:T(8,128)(2,1)}, u32[]{:S(2)}, u32[]{:S(2)}) collective-permute-start(bf16[768,4,128]{0,2,1:T(8,128)(2,1)} %bitcast.162), channel_id=1, source_target_pairs={{16,0},{20,4},{24,8},{28,12},{0,16},{4,20},{8,24},{12,28},{17,1},{... | collective-permute-start | bytes 2359304 | tf_op jit(solution)/shard_map/ppermute | solution.py:30
  1169.4 4.6 copy-start.11
Sparse Core Ops, SparseCore 0:
  905.2 117.8 all-gather.2
